TPU v7x, 32 devices: a whole 2x2x4 slice. The times are simulated.
32 devices in a mesh: lon: 8 (over y, x, core), spec: 4 (over z).
Axes of the slice: x: 2, y: 2, z: 4, core: 2. Of those that a mesh axis runs over, the one named last changes fastest.
Arguments:
- lam_final: float32 [1296, 64, 1024], P('spec', None, 'lon'), may hold values from -6 to 6
- stored_source: bfloat16 [2, 1296, 64, 1024], P(None, 'spec', None, 'lon'), may hold values from 0.19921875 to 1.1953125
- mixing: bfloat16 [1296, 1296], replicated, may hold values from -0.15625 to 0.15625
- drift_x: float32 [1296], replicated, may hold values from -0.45 to 0.45
- drift_y: float32 [1296], replicated, may hold values from -0.45 to 0.45
- ocean_mask: int32 [64, 1024], P(None, 'lon'), may hold values 0 or 1
- misfit: float32 [2, 64, 1024], P(None, None, 'lon'), may hold values from -6 to 6
- obs_mask: int32 [2, 64, 1024], P(None, None, 'lon'), may hold values 0 or 1
Outputs:
- lam_start: float32 [1296, 64, 1024], P('spec', None, 'lon')
All inputs are finite; a program needn't handle non-finite values. No bound on the sum of `ocean_mask` or of `obs_mask` on one device may be relied on, other than what follows from the above.
Results may differ from a plain program's by a relative error of at most 0.0028.
Values may be sent and summed in bfloat16 or wider, within the bound.
A program may use at most 192 MiB of HBM per device.

v0:
```python
import jax
import jax.numpy as jnp
from jax import lax
from jax.sharding import PartitionSpec as P

STEPS = 2


def with_halo(block, sides, width):
    for axis, dim in sides:
        count = lax.axis_size(axis)
        forward = [(i, i + 1) for i in range(count - 1)]
        forward.append((count - 1, 0))
        backward = [(target, source) for source, target in forward]
        low = lax.ppermute(
            lax.slice_in_dim(block, block.shape[dim] - width, None, axis=dim), axis, forward
        )
        high = lax.ppermute(lax.slice_in_dim(block, 0, width, axis=dim), axis, backward)
        block = jnp.concatenate([low, block, high], axis=dim)
    return block


def couple_local(rounded, mixing):
    flat = rounded.reshape(rounded.shape[0], -1)
    coupled = lax.dot_general(
        mixing, flat, (((0,), (0,)), ((), ())), preferred_element_type=jnp.float32
    )
    return coupled.astype(jnp.bfloat16).reshape(rounded.shape)


def advect_step(adjoint, speed_x, speed_y, northern, southern):
    padded = with_halo(adjoint, (("lon", 2),), 1)
    eastern = padded[:, :, 2:]
    western = padded[:, :, :-2]
    speed_x = speed_x[:, None, None]
    speed_y = speed_y[:, None, None]
    stay = 1.0 - jnp.abs(speed_x) - jnp.abs(speed_y)
    result = (
        stay * adjoint + jnp.maximum(speed_x, 0.0) * eastern + jnp.maximum(-speed_x, 0.0) * western
    )
    return result + jnp.maximum(speed_y, 0.0) * northern + jnp.maximum(-speed_y, 0.0) * southern


def per_device(lam_final, stored_source, mixing, drift_x, drift_y, ocean_mask, misfit, obs_mask):
    spec_index = lax.axis_index("spec")
    own_count = lam_final.shape[0]
    speed_x = lax.dynamic_slice_in_dim(drift_x, spec_index * own_count, own_count)
    speed_y = lax.dynamic_slice_in_dim(drift_y, spec_index * own_count, own_count)
    ocean_field = ocean_mask.astype(jnp.float32)[None]
    adjoint = lam_final
    for step_index in reversed(range(STEPS)):
        forcing = misfit[step_index] * obs_mask[step_index].astype(jnp.float32)
        adjoint = (adjoint + forcing[None]) * ocean_field
        rounded = adjoint.astype(jnp.bfloat16)
        coupled = couple_local(
            lax.all_to_all(rounded, "spec", split_axis=1, concat_axis=0, tiled=True), mixing
        )
        coupled = lax.all_to_all(coupled, "spec", split_axis=0, concat_axis=1, tiled=True)
        adjoint = adjoint + stored_source[step_index].astype(jnp.float32) * coupled.astype(
            jnp.float32
        )
        zero_row = jnp.zeros_like(adjoint[:, :1])
        northern = jnp.concatenate([adjoint[:, 1:], zero_row], axis=1)
        southern = jnp.concatenate([zero_row, adjoint[:, :-1]], axis=1)
        adjoint = advect_step(adjoint, speed_x, speed_y, northern, southern)
    return adjoint


def solution(mesh):
    in_specs = (
        P("spec", None, "lon"),
        P(None, "spec", None, "lon"),
        P(),
        P(),
        P(),
        P(None, "lon"),
        P(None, None, "lon"),
        P(None, None, "lon"),
    )
    out_specs = P("spec", None, "lon")
    return jax.shard_map(
        per_device, mesh=mesh, in_specs=in_specs, out_specs=out_specs, check_vma=False
    )
```

profile of v0, /device:TPU:0, one launch (start us, length us, event | category | flops | bytes accessed | tf_op | source)
XLA Modules:
  0.0 733.8 jit_solution(17673067778883216311)
XLA Ops:
  0.0 0.8 convert_element_type.66
  0.8 0.8 multiply_bitcast_fusion.1
  1.6 11.5 %fusion.17 = bf16[324,64,128]{2,0,1:T(8,128)(2,1)S(1)} fusion(f32[324,64,128]{2,1,0:T(8,128)} %param.8, f32[64,128]{1,0:T(8,128)S(1)} %convert_element_type.66, f32[64,128]{1,0:T(8,128)S(1)} %get-tuple-element.17), kind=kLoop, calls=%fused_computation.24 | loop fusion | flops 7962624 | bytes 15990784 | tf_op jit(solution)/shard_map/convert_element_type | solution.py:54
  13.1 0.0 copy-start.2
  13.1 125.0 %all_to_all.48 = bf16[324,64,128]{2,0,1:T(8,128)(2,1)S(1)} all-to-all(bf16[324,64,128]{2,0,1:T(8,128)(2,1)S(1)} %fusion.17), channel_id=1, replica_groups=mesh['lon'=8,'spec'=4] {'spec'}, dimensions={1} | all-to-all | bytes 10616832 | tf_op jit(solution)/shard_map/all_to_all | solution.py:56
  138.1 0.8 copy.17
  138.9 9.2 %fusion.22 = bf16[162,8,16,128]{3,1,2,0:T(8,128)(2,1)S(1)} fusion(bf16[1296,1296]{1,0:T(8,128)(2,1)S(1)} %copy-done.2, bf16[162,8,16,128]{3,2,1,0:T(8,128)(2,1)S(1)} %bitcast.67), kind=kOutput, calls=%fused_computation.33 | convolution fusion | flops 6882361344 | bytes 13976064 | tf_op jit(solution)/shard_map/dot_general | solution.py:25
  148.1 4.2 copy.34
  152.3 5.3 all-to-all-start.1
  157.6 0.8 abs_subtract_fusion
  158.4 10.6 %fusion.34 = (bf16[1,324,64,128]{3,2,1,0:T(8,128)(2,1)}, bf16[1,324,64,128]{3,2,1,0:T(8,128)(2,1)}) fusion(bf16[2,324,64,128]{3,2,1,0:T(8,128)(2,1)} %param.9), kind=kLoop, calls=%fused_computation.47 | loop fusion | bytes 21233664 | tf_op jit(solution)/shard_map/slice | solution.py:59
  169.0 104.8 %all-to-all-done.1 = bf16[1296,16,128]{2,1,0:T(8,128)(2,1)} async-done(((bf16[1296,16,128]{2,1,0:T(8,128)(2,1)}), bf16[1296,16,128]{2,1,0:T(8,128)(2,1)}, u32[]{:S(2)}, u32[]{:S(2)}) %all-to-all-start.1) | async-done | bytes 5308448 | tf_op jit(solution)/shard_map/all_to_all | solution.py:58
  273.8 3.7 copy.18
  277.5 0.1 slice-done.4
  277.6 12.9 %fusion.15 = f32[324,64,128]{2,0,1:T(8,128)S(1)} fusion(f32[4,324,16,128]{3,1,2,0:T(8,128)S(1)} %copy.18, f32[324,64,128]{2,1,0:T(8,128)} %param.8, bf16[1,324,64,128]{3,2,1,0:T(8,128)(2,1)S(1)} %bitcast.63, f32[64,128]{1,0:T(8,128)S(1)} %convert_element_type.66, f32[64,128]{1,0:T(8,128)S(1)} %get-tuple-element.17), kind=kLoop, calls=%fused_computation.21 | loop fusion | flops 13271040 | bytes 37224448 | tf_op jit(solution)/shard_map/add | solution.py:59
  290.5 9.5 %fusion.32 = (f32[324,64,1]{2,0,1:T(8,128)}, f32[324,64,1]{2,0,1:T(8,128)}) fusion(f32[324,64,128]{2,0,1:T(8,128)S(1)} %fusion.15), kind=kLoop, calls=%fused_computation.45 | loop fusion | bytes 331776 | tf_op jit(solution)/shard_map/slice | solution.py:18
  300.1 1.0 copy-done
  301.1 6.5 copy.19
  307.6 6.5 copy.21
  314.0 0.1 collective-permute-start.1
  314.1 3.0 collective-permute-start
  317.1 15.7 %fusion.33 = (f32[324,63,128]{2,0,1:T(8,128)}, f32[324,63,128]{2,0,1:T(8,128)}) fusion(f32[324,64,128]{2,0,1:T(8,128)} %copy-done), kind=kLoop, calls=%fused_computation.46 | loop fusion | bytes 41803776 | tf_op jit(solution)/shard_map/slice | solution.py:63
  332.8 0.0 collective-permute-done
  332.8 5.6 copy.20
  338.4 0.0 collective-permute-done.1
  338.4 5.6 copy.22
  344.0 30.8 %fusion.28 = (bf16[324,64,128]{2,0,1:T(8,128)(2,1)S(1)}, f32[324,64,128]{2,0,1:T(8,128)}) fusion(f32[64,128]{1,0:T(8,128)S(1)} %convert_element_type.66, f32[64,128]{1,0:T(8,128)S(1)} %get-tuple-element.18, f32[324,63,128]{2,0,1:T(8,128)} %get-tuple-element.14, f32[324]{0:T(512)S(1)} %get-tuple-element.23, f32[324,63,128]{2,0,1:T(8,128)} %get-tuple-element.13, ...), kind=kLoop, calls=%fused_computation.42 | loop fusion | flops 37158912 | bytes 47681872 | tf_op jit(solution)/shard_map/convert_element_type | solution.py:54
  374.8 121.0 %all_to_all.49 = bf16[324,64,128]{2,0,1:T(8,128)(2,1)S(1)} all-to-all(bf16[324,64,128]{2,0,1:T(8,128)(2,1)S(1)} %get-tuple-element.5), channel_id=1, replica_groups=mesh['lon'=8,'spec'=4] {'spec'}, dimensions={1} | all-to-all | bytes 10616832 | tf_op jit(solution)/shard_map/all_to_all | solution.py:56
  495.8 0.8 copy.24
  496.6 9.5 %fusion.25 = bf16[162,8,16,128]{3,1,2,0:T(8,128)(2,1)S(1)} fusion(bf16[1296,1296]{1,0:T(8,128)(2,1)S(1)} %copy-done.3, bf16[162,8,16,128]{3,2,1,0:T(8,128)(2,1)S(1)} %bitcast.68), kind=kOutput, calls=%fused_computation.34 | convolution fusion | flops 6882361344 | bytes 13976064 | tf_op jit(solution)/shard_map/dot_general | solution.py:25
  506.1 1.8 copy.36
  507.9 0.0 slice-start
  507.9 0.0 slice-start.1
  507.9 119.2 %all_to_all.50 = bf16[1296,16,128]{2,1,0:T(8,128)(2,1)S(1)} all-to-all(bf16[1296,16,128]{2,1,0:T(8,128)(2,1)S(1)} %bitcast.65), channel_id=1, replica_groups=mesh['lon'=8,'spec'=4] {'spec'}, dimensions={0} | all-to-all | bytes 10616832 | tf_op jit(solution)/shard_map/all_to_all | solution.py:58
  627.2 5.0 copy.25
  632.2 8.3 %fusion.14 = f32[324,64,128]{2,0,1:T(8,128)S(1)} fusion(f32[324,64,128]{2,0,1:T(8,128)S(1)} %bitcast.59, f32[4,324,16,128]{3,1,2,0:T(8,128)} %copy.25, bf16[1,324,64,128]{3,2,1,0:T(8,128)(2,1)} %get-tuple-element.15), kind=kLoop, calls=%fused_computation.19 | loop fusion | flops 7962624 | bytes 37158912 | tf_op jit(solution)/shard_map/add | solution.py:59
  640.5 9.4 %fusion.31 = (f32[324,64,1]{2,0,1:T(8,128)}, f32[324,64,1]{2,0,1:T(8,128)}) fusion(f32[324,64,128]{2,0,1:T(8,128)S(1)} %fusion.14), kind=kLoop, calls=%fused_computation.44 | loop fusion | bytes 331776 | tf_op jit(solution)/shard_map/slice | solution.py:18
  649.8 1.1 copy-done.1
  650.9 6.5 copy.26
  657.4 6.5 copy.28
  663.9 0.1 collective-permute-start.3
  664.0 2.6 collective-permute-start.2
  666.6 15.7 %fusion.30 = (f32[324,63,128]{2,0,1:T(8,128)}, f32[324,63,128]{2,0,1:T(8,128)}) fusion(f32[324,64,128]{2,0,1:T(8,128)} %copy-done.1), kind=kLoop, calls=%fused_computation.43 | loop fusion | bytes 41803776 | tf_op jit(solution)/shard_map/slice | solution.py:63
  682.3 0.0 collective-permute-done.2
  682.3 5.6 copy.27
  687.8 5.6 copy.29
  693.5 29.9 %fusion.3 = f32[324,64,128]{2,0,1:T(8,128)} fusion(f32[324,64,128]{2,0,1:T(8,128)} %copy-done.1, f32[324,64,1]{2,0,1:T(8,128)} %copy.29, f32[324,64,1]{2,0,1:T(8,128)} %copy.27, f32[324,63,128]{2,0,1:T(8,128)} %get-tuple-element.8, f32[324,63,128]{2,0,1:T(8,128)} %get-tuple-element.7, f32[324]{0:T(512)S(1)} %get-tuple-element.23, ...), kind=kLoop, calls=%fused_computation.4 | loop fusion | flops 29196288 | bytes 42307920 | tf_op jit(solution)/shard_map/add | solution.py:41
  723.4 10.2 %copy.30 = f32[324,64,128]{2,1,0:T(8,128)} copy(f32[324,64,128]{2,0,1:T(8,128)} %fusion.3) | data formatting | bytes 21233664 | tf_op jit(solution)/shard_map/add | solution.py:41
  (15 shorter events, 0.0 us)
Async XLA Ops:
  13.1 125.8 %copy-start.2 = (bf16[1296,1296]{1,0:T(8,128)(2,1)S(1)}, bf16[1296,1296]{1,0:T(8,128)(2,1)}, u32[]{:S(2)}) copy-start(bf16[1296,1296]{1,0:T(8,128)(2,1)} %param.10) | copy-start | bytes 10077700
  152.3 121.5 %all-to-all-start.1 = ((bf16[1296,16,128]{2,1,0:T(8,128)(2,1)}), bf16[1296,16,128]{2,1,0:T(8,128)(2,1)}, u32[]{:S(2)}, u32[]{:S(2)}) async-start(bf16[1296,16,128]{2,1,0:T(8,128)(2,1)} %bitcast.64), calls=%async_computation.1 | async-start | bytes 10616832 | tf_op jit(solution)/shard_map/all_to_all | solution.py:58
  169.0 108.5 %slice-start.3 = ((s8[5308416]{0:T(1024)(128)(4,1)}), s8[1114112]{0:T(1024)(128)(4,1)S(1)}, s32[]{:S(2)}) async-start(s8[5308416]{0:T(1024)(128)(4,1)} %bitcast.62), calls=%async_computation.7 | async-start | bytes 2228224
  273.8 3.8 slice-start.4
  290.5 10.6 %copy-start = (f32[324,64,128]{2,0,1:T(8,128)}, f32[324,64,128]{2,0,1:T(8,128)S(1)}, u32[]{:S(2)}) copy-start(f32[324,64,128]{2,0,1:T(8,128)S(1)} %fusion.15) | copy-start | bytes 31850500
  314.0 24.4 %collective-permute-start.1 = (f32[324,64,1]{0,1,2:T(8,128)S(1)}, f32[324,64,1]{0,1,2:T(8,128)S(1)}, u32[]{:S(2)}, u32[]{:S(2)}) collective-permute-start(f32[324,64,1]{0,1,2:T(8,128)S(1)} %copy.21), channel_id=1, source_target_pairs={{0,4},{4,8},{8,12},{12,16},{16,20},{20,24},{24,28},{28,0},{1,5},{5... | collective-permute-start | bytes 248840 | tf_op jit(solution)/shard_map/ppermute | solution.py:15
  314.1 18.7 %collective-permute-start = (f32[324,64,1]{0,1,2:T(8,128)S(1)}, f32[324,64,1]{0,1,2:T(8,128)S(1)}, u32[]{:S(2)}, u32[]{:S(2)}) collective-permute-start(f32[324,64,1]{0,1,2:T(8,128)S(1)} %copy.19), channel_id=1, source_target_pairs={{4,0},{8,4},{12,8},{16,12},{20,16},{24,20},{28,24},{0,28},{5,1},{9... | collective-permute-start | bytes 248840 | tf_op jit(solution)/shard_map/ppermute | solution.py:18
  374.8 121.8 %copy-start.3 = (bf16[1296,1296]{1,0:T(8,128)(2,1)S(1)}, bf16[1296,1296]{1,0:T(8,128)(2,1)}, u32[]{:S(2)}) copy-start(bf16[1296,1296]{1,0:T(8,128)(2,1)} %param.10) | copy-start | bytes 10077700
  507.9 124.2 %slice-start = ((s8[10747904]{0:T(1024)(128)(4,1)}), s8[4194304]{0:T(1024)(128)(4,1)S(1)}, s32[]{:S(2)}) async-start(s8[10747904]{0:T(1024)(128)(4,1)} %bitcast.58), calls=%async_computation.4 | async-start | bytes 8388608
  507.9 124.2 %slice-start.1 = ((s8[10747904]{0:T(1024)(128)(4,1)}), s8[4194304]{0:T(1024)(128)(4,1)S(1)}, s32[]{:S(2)}) async-start(s8[10747904]{0:T(1024)(128)(4,1)} %bitcast.58), calls=%async_computation.5 | async-start | bytes 8388608
  627.2 5.0 slice-start.2
  640.5 10.4 %copy-start.1 = (f32[324,64,128]{2,0,1:T(8,128)}, f32[324,64,128]{2,0,1:T(8,128)S(1)}, u32[]{:S(2)}) copy-start(f32[324,64,128]{2,0,1:T(8,128)S(1)} %fusion.14) | copy-start | bytes 31850500
  663.9 23.9 %collective-permute-start.3 = (f32[324,64,1]{0,1,2:T(8,128)S(1)}, f32[324,64,1]{0,1,2:T(8,128)S(1)}, u32[]{:S(2)}, u32[]{:S(2)}) collective-permute-start(f32[324,64,1]{0,1,2:T(8,128)S(1)} %copy.28), channel_id=1, source_target_pairs={{0,4},{4,8},{8,12},{12,16},{16,20},{20,24},{24,28},{28,0},{1,5},{5... | collective-permute-start | bytes 248840 | tf_op jit(solution)/shard_map/ppermute | solution.py:15
  664.0 18.3 %collective-permute-start.2 = (f32[324,64,1]{0,1,2:T(8,128)S(1)}, f32[324,64,1]{0,1,2:T(8,128)S(1)}, u32[]{:S(2)}, u32[]{:S(2)}) collective-permute-start(f32[324,64,1]{0,1,2:T(8,128)S(1)} %copy.26), channel_id=1, source_target_pairs={{4,0},{8,4},{12,8},{16,12},{20,16},{24,20},{28,24},{0,28},{5,1},{9... | collective-permute-start | bytes 248840 | tf_op jit(solution)/shard_map/ppermute | solution.py:18
where the time goes:
time: 740 us; the launch traced here: 734 us
  blocking collectives  365 us (49%)
  local copies, waits for them, and re-layouts  138 us (19%)
  waiting for transfers between devices  105 us (14%)
  other arithmetic  95.9 us (13%)
  matrix products  18.7 us (3%)
  starting transfers between devices  11 us (1%)
    all_to_all x2, blocking collectives, per_device(): lax.all_to_all(rounded, 'spec', split_axis=1, concat_axis=0, tiled=True)  246 us
    all_to_all x1, blocking collectives, per_device(): lax.all_to_all(coupled, 'spec', split_axis=0, concat_axis=1, tiled=True)  119 us
    all_to_all x1, waiting for transfers between devices, per_device(): lax.all_to_all(coupled, 'spec', split_axis=0, concat_axis=1, tiled=True)  105 us
    convert_element_type x2, other arithmetic, per_device(): rounded = adjoint.astype(jnp.bfloat16)  42.3 us
    slice x4, local copies, waits for them, and re-layouts, with_halo(): lax.slice_in_dim(block, 0, width, axis=dim)  31.8 us
    slice x2, local copies, waits for them, and re-layouts, per_device(): northern = jnp.concatenate([adjoint[:, 1:], zero_row], axis=1)  31.4 us
    add x1, other arithmetic, advect_step(): result + jnp.maximum(speed_y, 0.0) * northern  29.9 us
    add x2, other arithmetic, per_device(): adjoint + stored_source[step_index].astype(jnp.float32) * coupled.astype(...  21.3 us
  transfers between devices with their start and end apart: 5, of which 1 were waited for; matrix products, arithmetic and copies ran while one was open for 7% of the time, Pallas kernels for 0%

commit v1 on v0

--- a/solution.py
+++ b/solution.py
@@ -55,7 +55,9 @@
         coupled = couple_local(
             lax.all_to_all(rounded, "spec", split_axis=1, concat_axis=0, tiled=True), mixing
         )
-        coupled = lax.all_to_all(coupled, "spec", split_axis=0, concat_axis=1, tiled=True)
+        pieces = jnp.split(coupled, lax.axis_size("spec"), axis=0)
+        arrived = lax.all_to_all(jnp.stack(pieces), "spec", 0, 0)
+        coupled = jnp.concatenate(arrived, axis=1)
         adjoint = adjoint + stored_source[step_index].astype(jnp.float32) * coupled.astype(
             jnp.float32
         )

time: 740 us -> 772 us (1.043)
  other arithmetic: 95.9 us -> 116 us
  local copies, waits for them, and re-layouts: 138 us -> 150 us
    convert_element_type x0 -> x2, other arithmetic: none -> 13.8 us  [per_device(): coupled.astype(jnp.float32)]
    convert_element_type x2, local copies, waits for them, and re-layouts: 8.65 us -> 18.6 us  [per_device(): coupled.astype(jnp.float32)]
where the time goes in v1:
time: 772 us; the launch traced here: 765 us
  blocking collectives  365 us (47%)
  local copies, waits for them, and re-layouts  150 us (19%)
  other arithmetic  116 us (15%)
  waiting for transfers between devices  105 us (14%)
  matrix products  18.7 us (2%)
  starting transfers between devices  10.6 us (1%)
    all_to_all x2, blocking collectives, per_device(): lax.all_to_all(rounded, 'spec', split_axis=1, concat_axis=0, tiled=True)  246 us
    all_to_all x1, blocking collectives, per_device(): arrived = lax.all_to_all(jnp.stack(pieces), 'spec', 0, 0)  119 us
    all_to_all x1, waiting for transfers between devices, per_device(): arrived = lax.all_to_all(jnp.stack(pieces), 'spec', 0, 0)  105 us
    convert_element_type x2, other arithmetic, per_device(): rounded = adjoint.astype(jnp.bfloat16)  42.3 us
    slice x4, local copies, waits for them, and re-layouts, with_halo(): lax.slice_in_dim(block, 0, width, axis=dim)  32.1 us
    slice x2, local copies, waits for them, and re-layouts, per_device(): northern = jnp.concatenate([adjoint[:, 1:], zero_row], axis=1)  31.6 us
    add x1, other arithmetic, advect_step(): result + jnp.maximum(speed_y, 0.0) * northern  29.9 us
    add x2, other arithmetic, per_device(): adjoint + stored_source[step_index].astype(jnp.float32) * coupled.astype(...  24 us
  transfers between devices with their start and end apart: 5, of which 1 were waited for; matrix products, arithmetic and copies ran while one was open for 7% of the time, Pallas kernels for 0%

profile of v1, /device:TPU:0, one launch (start us, length us, event | category | flops | bytes accessed | tf_op | source)
XLA Modules:
  0.0 765.4 jit_solution(11980220299925466079)
XLA Ops:
  0.0 0.8 convert_element_type.60
  0.8 0.8 multiply_bitcast_fusion.1
  1.6 11.5 %fusion.17 = bf16[324,64,128]{2,0,1:T(8,128)(2,1)S(1)} fusion(f32[324,64,128]{2,1,0:T(8,128)} %param.8, f32[64,128]{1,0:T(8,128)S(1)} %convert_element_type.60, f32[64,128]{1,0:T(8,128)S(1)} %get-tuple-element.25), kind=kLoop, calls=%fused_computation.26 | loop fusion | flops 7962624 | bytes 15990784 | tf_op jit(solution)/shard_map/convert_element_type | solution.py:54
  13.1 125.0 %all_to_all.40 = bf16[324,64,128]{2,0,1:T(8,128)(2,1)S(1)} all-to-all(bf16[324,64,128]{2,0,1:T(8,128)(2,1)S(1)} %fusion.17), channel_id=1, replica_groups=mesh['lon'=8,'spec'=4] {'spec'}, dimensions={1} | all-to-all | bytes 10616832 | tf_op jit(solution)/shard_map/all_to_all | solution.py:56
  138.1 0.8 copy.17
  138.9 9.2 %fusion.18 = bf16[1296,2048]{1,0:T(8,128)(2,1)S(1)} fusion(bf16[1296,1296]{1,0:T(8,128)(2,1)S(1)} %copy-done.2, bf16[162,8,16,128]{3,2,1,0:T(8,128)(2,1)S(1)} %bitcast.102), kind=kOutput, calls=%fused_computation.29 | convolution fusion | flops 6882361344 | bytes 13976064 | tf_op jit(solution)/shard_map/dot_general | solution.py:25
  148.1 1.0 fusion.32
  149.5 0.3 copy.37
  149.8 0.3 copy.36
  150.4 0.7 slice_bitcast_fusion.4
  151.1 0.5 slice_bitcast_fusion.6
  151.6 2.9 pad_maximum_fusion.4
  154.5 5.3 all-to-all-start.1
  159.7 0.8 abs_subtract_fusion
  160.5 10.6 %fusion.30 = (bf16[1,324,64,128]{3,2,1,0:T(8,128)(2,1)}, bf16[1,324,64,128]{3,2,1,0:T(8,128)(2,1)}) fusion(bf16[2,324,64,128]{3,2,1,0:T(8,128)(2,1)} %param.9), kind=kLoop, calls=%fused_computation.59 | loop fusion | bytes 21233664 | tf_op jit(solution)/shard_map/slice | solution.py:61
  171.1 104.8 %all-to-all-done.1 = bf16[4,324,16,128]{3,2,1,0:T(8,128)(2,1)} async-done(((bf16[4,324,16,128]{3,2,1,0:T(8,128)(2,1)}), bf16[4,324,16,128]{3,2,1,0:T(8,128)(2,1)}, u32[]{:S(2)}, u32[]{:S(2)}) %all-to-all-start.1) | async-done | bytes 5308448 | tf_op jit(solution)/shard_map/all_to_all | solution.py:59
  275.9 7.5 convert_bitcast_fusion.1
  283.5 7.3 copy.18
  290.7 16.0 %fusion.15 = f32[324,64,128]{2,0,1:T(8,128)S(1)} fusion(f32[324,4,16,128]{3,0,2,1:T(8,128)S(1)} %copy.18, f32[324,64,128]{2,1,0:T(8,128)} %param.8, bf16[1,324,64,128]{3,2,1,0:T(8,128)(2,1)} %get-tuple-element.16, f32[64,128]{1,0:T(8,128)S(1)} %convert_element_type.60, f32[64,128]{1,0:T(8,128)S(1)} %get-tuple-element.25), kind=kLoop, calls=%fused_computation.21 | loop fusion | flops 13271040 | bytes 37224448 | tf_op jit(solution)/shard_map/add | solution.py:61
  306.8 9.8 %fusion.28 = (f32[324,64,1]{2,0,1:T(8,128)}, f32[324,64,1]{2,0,1:T(8,128)}) fusion(f32[324,64,128]{2,0,1:T(8,128)S(1)} %fusion.15), kind=kLoop, calls=%fused_computation.57 | loop fusion | bytes 331776 | tf_op jit(solution)/shard_map/slice | solution.py:18
  316.6 0.7 copy-done
  317.3 6.5 copy.19
  323.7 6.5 copy.21
  330.3 2.6 collective-permute-start
  332.9 15.7 %fusion.29 = (f32[324,63,128]{2,0,1:T(8,128)}, f32[324,63,128]{2,0,1:T(8,128)}) fusion(f32[324,64,128]{2,0,1:T(8,128)} %copy-done), kind=kLoop, calls=%fused_computation.58 | loop fusion | bytes 41803776 | tf_op jit(solution)/shard_map/slice | solution.py:65
  348.6 5.6 copy.20
  354.2 5.6 copy.22
  359.8 30.8 %fusion.24 = (bf16[324,64,128]{2,0,1:T(8,128)(2,1)S(1)}, f32[324,64,128]{2,0,1:T(8,128)}) fusion(f32[64,128]{1,0:T(8,128)S(1)} %convert_element_type.60, f32[64,128]{1,0:T(8,128)S(1)} %get-tuple-element.26, f32[324,63,128]{2,0,1:T(8,128)} %get-tuple-element.14, f32[324]{0:T(512)S(1)} %get-tuple-element.31, f32[324,63,128]{2,0,1:T(8,128)} %get-tuple-element.13, ...), kind=kLoop, calls=%fused_computation.54 | loop fusion | flops 37158912 | bytes 47681872 | tf_op jit(solution)/shard_map/convert_element_type | solution.py:54
  390.6 121.2 %all_to_all.41 = bf16[324,64,128]{2,0,1:T(8,128)(2,1)S(1)} all-to-all(bf16[324,64,128]{2,0,1:T(8,128)(2,1)S(1)} %get-tuple-element.5), channel_id=1, replica_groups=mesh['lon'=8,'spec'=4] {'spec'}, dimensions={1} | all-to-all | bytes 10616832 | tf_op jit(solution)/shard_map/all_to_all | solution.py:56
  511.8 0.8 copy.24
  512.6 1.3 copy-done.3
  513.9 9.5 %fusion.19 = bf16[1296,2048]{1,0:T(8,128)(2,1)S(1)} fusion(bf16[1296,1296]{1,0:T(8,128)(2,1)S(1)} %copy-done.3, bf16[162,8,16,128]{3,2,1,0:T(8,128)(2,1)S(1)} %bitcast.103), kind=kOutput, calls=%fused_computation.30 | convolution fusion | flops 6882361344 | bytes 13976064 | tf_op jit(solution)/shard_map/dot_general | solution.py:25
  523.3 1.0 fusion.31
  526.6 0.7 pad_maximum_fusion.5
  527.3 118.9 %all_to_all.42 = bf16[4,324,16,128]{3,2,1,0:T(8,128)(2,1)S(1)} all-to-all(bf16[4,324,16,128]{3,2,1,0:T(8,128)(2,1)S(1)} %pad_maximum_fusion.5), channel_id=1, replica_groups=mesh['lon'=8,'spec'=4] {'spec'}, dimensions={0} | all-to-all | bytes 10616832 | tf_op jit(solution)/shard_map/all_to_all | solution.py:59
  646.2 6.3 convert_bitcast_fusion
  652.5 11.3 %copy.25 = f32[324,4,16,128]{3,0,2,1:T(8,128)} copy(f32[324,4,16,128]{3,2,0,1:T(8,128)} %convert_bitcast_fusion) | data formatting | bytes 21233664 | tf_op jit(solution)/shard_map/convert_element_type | solution.py:61
  663.9 8.0 %fusion.14 = f32[324,64,128]{2,0,1:T(8,128)S(1)} fusion(f32[324,64,128]{2,0,1:T(8,128)S(1)} %bitcast.83, f32[324,4,16,128]{3,0,2,1:T(8,128)} %copy.25, bf16[1,324,64,128]{3,2,1,0:T(8,128)(2,1)} %get-tuple-element.15), kind=kLoop, calls=%fused_computation.19 | loop fusion | flops 7962624 | bytes 37158912 | tf_op jit(solution)/shard_map/add | solution.py:61
  671.9 9.4 %fusion.27 = (f32[324,64,1]{2,0,1:T(8,128)}, f32[324,64,1]{2,0,1:T(8,128)}) fusion(f32[324,64,128]{2,0,1:T(8,128)S(1)} %fusion.14), kind=kLoop, calls=%fused_computation.56 | loop fusion | bytes 331776 | tf_op jit(solution)/shard_map/slice | solution.py:18
  681.2 1.1 copy-done.1
  682.3 6.5 copy.26
  688.8 6.5 copy.28
  695.3 2.6 collective-permute-start.2
  698.0 15.9 %fusion.26 = (f32[324,63,128]{2,0,1:T(8,128)}, f32[324,63,128]{2,0,1:T(8,128)}) fusion(f32[324,64,128]{2,0,1:T(8,128)} %copy-done.1), kind=kLoop, calls=%fused_computation.55 | loop fusion | bytes 41803776 | tf_op jit(solution)/shard_map/slice | solution.py:65
  713.8 5.6 copy.27
  719.4 5.6 copy.29
  725.0 29.9 %fusion.3 = f32[324,64,128]{2,0,1:T(8,128)} fusion(f32[324,64,128]{2,0,1:T(8,128)} %copy-done.1, f32[324,64,1]{2,0,1:T(8,128)} %copy.29, f32[324,64,1]{2,0,1:T(8,128)} %copy.27, f32[324,63,128]{2,0,1:T(8,128)} %get-tuple-element.8, f32[324,63,128]{2,0,1:T(8,128)} %get-tuple-element.7, f32[324]{0:T(512)S(1)} %get-tuple-element.31, ...), kind=kLoop, calls=%fused_computation.4 | loop fusion | flops 29196288 | bytes 42307920 | tf_op jit(solution)/shard_map/add | solution.py:41
  755.0 10.2 %copy.30 = f32[324,64,128]{2,1,0:T(8,128)} copy(f32[324,64,128]{2,0,1:T(8,128)} %fusion.3) | data formatting | bytes 21233664 | tf_op jit(solution)/shard_map/add | solution.py:41
  (28 shorter events, 2.9 us)
Async XLA Ops:
  13.1 125.8 %copy-start.2 = (bf16[1296,1296]{1,0:T(8,128)(2,1)S(1)}, bf16[1296,1296]{1,0:T(8,128)(2,1)}, u32[]{:S(2)}) copy-start(bf16[1296,1296]{1,0:T(8,128)(2,1)} %param.10) | copy-start | bytes 10077700
  154.5 121.5 %all-to-all-start.1 = ((bf16[4,324,16,128]{3,2,1,0:T(8,128)(2,1)}), bf16[4,324,16,128]{3,2,1,0:T(8,128)(2,1)}, u32[]{:S(2)}, u32[]{:S(2)}) async-start(bf16[4,324,16,128]{3,2,1,0:T(8,128)(2,1)} %pad_maximum_fusion.4), calls=%async_computation.1 | async-start | bytes 10616832 | tf_op jit(solution)/shard_map/all_to_all | solution.py:59
  306.8 10.5 %copy-start = (f32[324,64,128]{2,0,1:T(8,128)}, f32[324,64,128]{2,0,1:T(8,128)S(1)}, u32[]{:S(2)}) copy-start(f32[324,64,128]{2,0,1:T(8,128)S(1)} %fusion.15) | copy-start | bytes 31850500
  330.2 24.0 %collective-permute-start.1 = (f32[324,64,1]{0,1,2:T(8,128)S(1)}, f32[324,64,1]{0,1,2:T(8,128)S(1)}, u32[]{:S(2)}, u32[]{:S(2)}) collective-permute-start(f32[324,64,1]{0,1,2:T(8,128)S(1)} %copy.21), channel_id=1, source_target_pairs={{0,4},{4,8},{8,12},{12,16},{16,20},{20,24},{24,28},{28,0},{1,5},{5... | collective-permute-start | bytes 248840 | tf_op jit(solution)/shard_map/ppermute | solution.py:15
  330.3 18.4 %collective-permute-start = (f32[324,64,1]{0,1,2:T(8,128)S(1)}, f32[324,64,1]{0,1,2:T(8,128)S(1)}, u32[]{:S(2)}, u32[]{:S(2)}) collective-permute-start(f32[324,64,1]{0,1,2:T(8,128)S(1)} %copy.19), channel_id=1, source_target_pairs={{4,0},{8,4},{12,8},{16,12},{20,16},{24,20},{28,24},{0,28},{5,1},{9... | collective-permute-start | bytes 248840 | tf_op jit(solution)/shard_map/ppermute | solution.py:18
  511.8 2.0 copy-start.3
  646.2 17.6 %slice-start = ((s8[10747904]{0:T(1024)(128)(4,1)}), s8[4194304]{0:T(1024)(128)(4,1)S(1)}, s32[]{:S(2)}) async-start(s8[10747904]{0:T(1024)(128)(4,1)} %bitcast.82), calls=%async_computation.4 | async-start | bytes 8388608
  646.2 17.6 %slice-start.1 = ((s8[10747904]{0:T(1024)(128)(4,1)}), s8[4194304]{0:T(1024)(128)(4,1)S(1)}, s32[]{:S(2)}) async-start(s8[10747904]{0:T(1024)(128)(4,1)} %bitcast.82), calls=%async_computation.5 | async-start | bytes 8388608
  652.5 11.4 %slice-start.2 = ((s8[10747904]{0:T(1024)(128)(4,1)}), s8[2359296]{0:T(1024)(128)(4,1)S(1)}, s32[]{:S(2)}) async-start(s8[10747904]{0:T(1024)(128)(4,1)} %bitcast.82), calls=%async_computation.6 | async-start | bytes 4718592
  671.9 10.4 %copy-start.1 = (f32[324,64,128]{2,0,1:T(8,128)}, f32[324,64,128]{2,0,1:T(8,128)S(1)}, u32[]{:S(2)}) copy-start(f32[324,64,128]{2,0,1:T(8,128)S(1)} %fusion.14) | copy-start | bytes 31850500
  695.3 24.1 %collective-permute-start.3 = (f32[324,64,1]{0,1,2:T(8,128)S(1)}, f32[324,64,1]{0,1,2:T(8,128)S(1)}, u32[]{:S(2)}, u32[]{:S(2)}) collective-permute-start(f32[324,64,1]{0,1,2:T(8,128)S(1)} %copy.28), channel_id=1, source_target_pairs={{0,4},{4,8},{8,12},{12,16},{16,20},{20,24},{24,28},{28,0},{1,5},{5... | collective-permute-start | bytes 248840 | tf_op jit(solution)/shard_map/ppermute | solution.py:15
  695.3 18.5 %collective-permute-start.2 = (f32[324,64,1]{0,1,2:T(8,128)S(1)}, f32[324,64,1]{0,1,2:T(8,128)S(1)}, u32[]{:S(2)}, u32[]{:S(2)}) collective-permute-start(f32[324,64,1]{0,1,2:T(8,128)S(1)} %copy.26), channel_id=1, source_target_pairs={{4,0},{8,4},{12,8},{16,12},{20,16},{24,20},{28,24},{0,28},{5,1},{9... | collective-permute-start | bytes 248840 | tf_op jit(solution)/shard_map/ppermute | solution.py:18
